TPU v7x, 32 devices: a whole 2x2x4 slice. The times are simulated.
32 devices in a mesh: gx: 4 (over y, core), gy: 8 (over z, x).
Axes of the slice: x: 2, y: 2, z: 4, core: 2. Of those that a mesh axis runs over, the one named last changes fastest.
Arguments:
- tokens: bfloat16 [256, 8192], P('gy', 'gx'), may hold values from -12 to 12
- w_gate: bfloat16 [8192, 28672], P('gx', 'gy'), may hold values from -0.0625 to 0.0625
- w_up: bfloat16 [8192, 28672], P('gx', 'gy'), may hold values from -0.0625 to 0.0625
- w_down: bfloat16 [28672, 8192], P('gy', 'gx'), may hold values from -0.03125 to 0.03125
- w_head: bfloat16 [8192, 1024], P('gx'), may hold values from -0.0625 to 0.0625
- partner: int32 [256], replicated, may hold values from 0 to 255, as said below
Outputs:
- block_out: bfloat16 [256, 8192], P('gy', 'gx')
- pair_loss: float32 [], replicated
- grad_gate: bfloat16 [8192, 28672], P('gx', 'gy')
- grad_up: bfloat16 [8192, 28672], P('gx', 'gy')
- grad_down: bfloat16 [28672, 8192], P('gy', 'gx')
- grad_head: bfloat16 [8192, 1024], P('gx', 'gy')
Inputs may be any that keep to these rules, and one draw needn't show every extreme that they name: partner[i] differs from i, and every token is the partner of exactly one token.
All inputs are finite; a program needn't handle non-finite values.
Results may differ from a plain program's by a relative error of at most 0.029.
Values may be sent and summed in bfloat16 or wider, within the bound.
A program may use at most 256 MiB of HBM per device.

v0:
```python
import math
import jax
import jax.numpy as jnp
from jax import lax
from jax.sharding import PartitionSpec as P


def contract_lead(left_mat, right_mat):
    return lax.dot_general(
        left_mat, right_mat, (((0,), (0,)), ((), ())), preferred_element_type=jnp.float32
    )


def contract_last(left_mat, right_mat):
    return lax.dot_general(
        left_mat, right_mat, (((1,), (1,)), ((), ())), preferred_element_type=jnp.float32
    )


def score_rows(proj_all, partner, row_count, score_scale):
    token_count = proj_all.shape[0]
    scores = contract_last(proj_all, proj_all) * score_scale
    row_ids = jnp.arange(row_count, dtype=jnp.int32)
    col_ids = jnp.arange(token_count, dtype=jnp.int32)
    scores = jnp.where(row_ids[:, None] == col_ids[None, :], -jnp.inf, scores)
    row_max = jnp.max(scores, axis=1, keepdims=True)
    log_total = row_max[:, 0] + jnp.log(jnp.sum(jnp.exp(scores - row_max), axis=1))
    is_partner = col_ids[None, :] == partner[:, None]
    positive = jnp.sum(jnp.where(is_partner, scores, 0.0), axis=1)
    weights_grad = (jnp.exp(scores - log_total[:, None]) - is_partner.astype(jnp.float32)).astype(
        jnp.bfloat16
    )
    return (weights_grad, log_total - positive)


def per_device(tokens, w_gate, w_up, w_down, w_head, partner):
    tok_share = tokens.shape[0]
    head_width = w_head.shape[1]
    score_scale = 1.0 / math.sqrt(head_width)
    rows_all = lax.all_gather(tokens, "gy", axis=0, tiled=True)
    token_count = rows_all.shape[0]
    row_share = token_count // lax.axis_size("gx")
    x_first = lax.axis_index("gx") * row_share
    gate_all, up_all = (
        lax.psum(
            jnp.dot(rows_all, w_gate, preferred_element_type=jnp.float32).astype(jnp.bfloat16), "gx"
        ).astype(jnp.float32),
        lax.psum(
            jnp.dot(rows_all, w_up, preferred_element_type=jnp.float32).astype(jnp.bfloat16), "gx"
        ).astype(jnp.float32),
    )
    hidden_all = (gate_all * jax.nn.sigmoid(gate_all) * up_all).astype(jnp.bfloat16)
    gate_mine = lax.dynamic_slice_in_dim(gate_all, x_first, row_share, 0)
    up_mine = lax.dynamic_slice_in_dim(up_all, x_first, row_share, 0)
    picked = hidden_all
    down_out = lax.psum_scatter(
        jnp.dot(picked, w_down, preferred_element_type=jnp.float32).astype(jnp.bfloat16),
        "gy",
        scatter_dimension=0,
        tiled=True,
    ).astype(jnp.float32)
    block_out = (tokens.astype(jnp.float32) + down_out).astype(jnp.bfloat16)
    projected = lax.psum(
        jnp.dot(block_out, w_head, preferred_element_type=jnp.float32).astype(jnp.bfloat16), "gx"
    )
    proj_all = lax.all_gather(projected, "gy", axis=0, tiled=True)
    first_row = lax.axis_index("gy") * tok_share
    weights_all, row_loss = score_rows(proj_all, partner, token_count, score_scale)
    mine_rows = lax.dynamic_slice_in_dim(weights_all, first_row, tok_share, 0)
    mine_cols = lax.dynamic_slice_in_dim(weights_all, first_row, tok_share, 1)
    row_part = jnp.dot(mine_rows, proj_all, preferred_element_type=jnp.float32)
    column_part = contract_lead(mine_cols, proj_all)
    pair_loss = jnp.sum(row_loss) / token_count
    grad_proj = ((row_part + column_part) * score_scale).astype(jnp.bfloat16)
    grad_block = contract_last(grad_proj, w_head).astype(jnp.bfloat16)
    grad_head = lax.psum_scatter(
        contract_lead(block_out, grad_proj).astype(jnp.bfloat16),
        "gy",
        scatter_dimension=1,
        tiled=True,
    )
    block_grads = lax.all_gather(grad_block, "gy", axis=0, tiled=True)
    grad_down = contract_lead(hidden_all, block_grads).astype(jnp.bfloat16)
    picked = block_grads
    grad_hidden = lax.psum_scatter(
        contract_last(picked, w_down).astype(jnp.bfloat16), "gx", scatter_dimension=0, tiled=True
    ).astype(jnp.float32)
    sigmoid_gate = jax.nn.sigmoid(gate_mine)
    grad_gate_pre = (
        grad_hidden * up_mine * sigmoid_gate * (1.0 + gate_mine * (1.0 - sigmoid_gate))
    ).astype(jnp.bfloat16)
    grad_up_pre = (grad_hidden * gate_mine * sigmoid_gate).astype(jnp.bfloat16)
    gate_grads, up_grads = (
        lax.all_gather(grad_gate_pre, "gx", axis=0, tiled=True),
        lax.all_gather(grad_up_pre, "gx", axis=0, tiled=True),
    )
    grad_gate = contract_lead(rows_all, gate_grads).astype(jnp.bfloat16)
    grad_up = contract_lead(rows_all, up_grads).astype(jnp.bfloat16)
    return (block_out, pair_loss, grad_gate, grad_up, grad_down, grad_head)


def solution(mesh):
    in_specs = (P("gy", "gx"), P("gx", "gy"), P("gx", "gy"), P("gy", "gx"), P("gx", None), P())
    out_specs = (P("gy", "gx"), P(), P("gx", "gy"), P("gx", "gy"), P("gy", "gx"), P("gx", "gy"))
    return jax.shard_map(
        per_device, mesh=mesh, in_specs=in_specs, out_specs=out_specs, check_vma=False
    )
```

profile of v0, /device:TPU:0, one launch (start us, length us, event | category | flops | bytes accessed | tf_op | source)
XLA Modules:
  0.0 527.0 jit_solution(3588408594306243018)
XLA Ops:
  7.2 0.0 all-gather.5.cloned.1.call-start
  7.2 0.7 all-gather.5.cloned.1.call-update
  7.9 0.0 all-reduce.6.cloned.1.call-start
  7.9 45.1 %all-gather.5.cloned.1.call-done = bf16[256,2048]{1,0:T(8,128)(2,1)} async-done(((bf16[32,2048]{1,0:T(8,128)(2,1)}), bf16[256,2048]{1,0:T(8,128)(2,1)}) %all-gather.5.cloned.1.call-update) | async-done | bytes 1048592 | tf_op jit(solution)/shard_map/all_gather | solution.py:40
  53.0 10.8 %convolution_convert_fusion.4 = bf16[256,3584]{1,0:T(8,128)(2,1)} fusion(bf16[256,2048]{1,0:T(8,128)(2,1)} %all-gather.5.cloned.1.call-done, bf16[2048,3584]{1,0:T(8,128)(2,1)} %param.8), kind=kOutput, calls=%fused_computation.6 | convolution fusion | flops 3759013888 | bytes 17563648 | tf_op jit(solution)/shard_map/dot_general | solution.py:49
  63.8 10.3 %convolution_convert_fusion.5 = bf16[256,3584]{1,0:T(8,128)(2,1)} fusion(bf16[256,2048]{1,0:T(8,128)(2,1)S(1)} %copy-done, bf16[2048,3584]{1,0:T(8,128)(2,1)} %param.7), kind=kOutput, calls=%fused_computation.7 | convolution fusion | flops 3759013888 | bytes 17563648 | tf_op jit(solution)/shard_map/dot_general | solution.py:46
  74.0 0.0 all-reduce.6.cloned.1.call-update
  74.1 0.0 reduce-scatter.6.cloned.1.call-start
  74.1 76.0 %all-reduce.6.cloned.1.call-done = (bf16[256,3584]{1,0:T(8,128)(2,1)}, bf16[256,3584]{1,0:T(8,128)(2,1)}) async-done(((bf16[256,3584]{1,0:T(8,128)(2,1)}, bf16[256,3584]{1,0:T(8,128)(2,1)}), (bf16[256,3584]{1,0:T(8,128)(2,1)}, bf16[256,3584]{1,0:T(8,128)(2,1)})) %all-reduce.6.cloned.1.call-update) | async-done | bytes 3670032 | tf_op jit(solution)/shard_map/psum | solution.py:48
  150.1 11.6 %convolution_convert_fusion.7 = bf16[256,2048]{1,0:T(8,128)(2,1)} fusion(bf16[3584,2048]{1,0:T(8,128)(2,1)} %param.9, bf16[256,3584]{1,0:T(8,128)(2,1)} %get-tuple-element.20, bf16[256,3584]{1,0:T(8,128)(2,1)} %get-tuple-element.21), kind=kOutput, calls=%fused_computation.10 | convolution fusion | flops 3765960704 | bytes 19398656 | tf_op jit(solution)/shard_map/dot_general | solution.py:57
  161.8 0.0 all-reduce.4.cloned.1.call-start
  161.8 63.7 %reduce-scatter.6.cloned.1.call-done = bf16[32,2048]{1,0:T(8,128)(2,1)} async-done(((bf16[256,2048]{1,0:T(8,128)(2,1)}), bf16[32,2048]{1,0:T(8,128)(2,1)}) %reduce-scatter.6.cloned.1.call-update) | async-done | bytes 131088 | tf_op jit(solution)/shard_map/reduce_scatter | solution.py:56
  225.5 0.9 add_convert_fusion
  226.5 3.7 convolution_convert_fusion.9
  230.2 0.0 all-reduce.4.cloned.1.call-update
  230.2 0.0 all-gather.7.cloned.1.call-start
  230.2 30.1 %all-reduce.4.cloned.1.call-done = bf16[32,1024]{1,0:T(8,128)(2,1)} async-done(((bf16[32,1024]{1,0:T(8,128)(2,1)}), bf16[32,1024]{1,0:T(8,128)(2,1)}) %all-reduce.4.cloned.1.call-update) | async-done | bytes 65552 | tf_op jit(solution)/shard_map/psum | solution.py:63
  260.4 31.6 %all_gather.16 = bf16[256,1024]{1,0:T(8,128)(2,1)S(1)} all-gather(bf16[32,1024]{1,0:T(8,128)(2,1)} %all-reduce.4.cloned.1.call-done), channel_id=1, replica_groups=mesh['gx'=4,'gy'=8] {'gy'}, dimensions={0}, use_global_device_ids=true | all-gather | bytes 589824 | tf_op jit(solution)/shard_map/all_gather | solution.py:66
  292.0 0.4 fusion.15
  292.3 0.1 select_reduce_fusion
  292.4 0.6 subtract_reduce_fusion
  293.0 0.1 subtract_convert_fusion
  293.1 0.3 fusion.10
  293.4 0.2 fusion.4
  293.6 4.2 convolution_convert_fusion.8
  297.8 0.0 all-gather.7.cloned.1.call-update
  297.8 0.2 reduce-scatter.8.cloned.1.call-start
  298.0 40.0 %all-gather.7.cloned.1.call-done = bf16[256,2048]{1,0:T(8,128)(2,1)} async-done(((bf16[32,2048]{1,0:T(8,128)(2,1)}), bf16[256,2048]{1,0:T(8,128)(2,1)}) %all-gather.7.cloned.1.call-update) | async-done | bytes 1048592 | tf_op jit(solution)/shard_map/all_gather | solution.py:82
  338.0 10.7 %convolution_convert_fusion.3 = bf16[256,3584]{1,0:T(8,128)(2,1)} fusion(bf16[256,2048]{1,0:T(8,128)(2,1)} %all-gather.7.cloned.1.call-done, bf16[3584,2048]{1,0:T(8,128)(2,1)} %param.9), kind=kOutput, calls=%fused_computation.5 | convolution fusion | flops 3759013888 | bytes 17563648 | tf_op jit(solution)/shard_map/dot_general | solution.py:15
  348.8 0.0 all-gather.9.cloned.1.call-start
  348.8 3.9 convert_element_type.74
  352.7 2.3 convert_element_type.76
  355.0 22.5 %reduce-scatter.8.cloned.1.call-done = bf16[64,3584]{1,0:T(8,128)(2,1)} async-done(((bf16[256,3584]{1,0:T(8,128)(2,1)}), bf16[64,3584]{1,0:T(8,128)(2,1)}) %reduce-scatter.8.cloned.1.call-update) | async-done | bytes 458768 | tf_op jit(solution)/shard_map/reduce_scatter | solution.py:85
  377.5 2.9 fusion.9
  380.4 0.0 all-gather.9.cloned.1.call-update
  380.4 0.0 all-gather.11.cloned.1.call-start
  380.5 0.7 all-gather.11.cloned.1.call-update
  381.2 0.0 reduce-scatter.10.cloned.1.call-start
  381.3 3.3 convolution_convert_fusion.6
  384.5 6.5 %copy.16 = bf16[2048,1024]{0,1:T(8,128)(2,1)} copy(bf16[2048,1024]{1,0:T(8,128)(2,1)} %convolution_convert_fusion.6) | data formatting | bytes 8388608
  391.1 0.0 reduce-scatter.10.cloned.1.call-update
  391.7 11.7 %convolution_convert_fusion = bf16[3584,2048]{1,0:T(8,128)(2,1)} fusion(bf16[256,2048]{1,0:T(8,128)(2,1)} %all-gather.7.cloned.1.call-done, bf16[256,3584]{1,0:T(8,128)(2,1)S(1)} %copy-done.1, bf16[256,3584]{1,0:T(8,128)(2,1)} %get-tuple-element.21), kind=kOutput, calls=%fused_computation | convolution fusion | flops 3772776448 | bytes 19398656 | tf_op jit(solution)/shard_map/dot_general | solution.py:9
  403.5 9.1 %fusion = bf16[2048,3584]{0,1:T(8,128)(2,1)} fusion(bf16[256,3584]{1,0:T(8,128)(2,1)} %all-gather.9.cloned.1.call-done, bf16[256,2048]{1,0:T(8,128)(2,1)S(1)} %copy-done), kind=kOutput, calls=%fused_computation.3 | convolution fusion | flops 3765436416 | bytes 17563648 | tf_op jit(solution)/shard_map/dot_general | solution.py:9
  412.5 18.7 %copy.14 = bf16[2048,3584]{1,0:T(8,128)(2,1)} copy(bf16[2048,3584]{0,1:T(8,128)(2,1)} %fusion) | data formatting | bytes 29360128
  431.2 8.8 %fusion.1 = bf16[2048,3584]{0,1:T(8,128)(2,1)} fusion(bf16[256,3584]{1,0:T(8,128)(2,1)} %all-gather.11.cloned.1.call-done, bf16[256,2048]{1,0:T(8,128)(2,1)S(1)} %copy-done), kind=kOutput, calls=%fused_computation.4 | convolution fusion | flops 3765436416 | bytes 17563648 | tf_op jit(solution)/shard_map/dot_general | solution.py:9
  440.0 18.8 %copy.15 = bf16[2048,3584]{1,0:T(8,128)(2,1)} copy(bf16[2048,3584]{0,1:T(8,128)(2,1)} %fusion.1) | data formatting | bytes 29360128
  458.7 58.6 %reduce-scatter.10.cloned.1.call-done = bf16[128,2048]{1,0:T(8,128)(2,1)} async-done(((bf16[1024,2048]{1,0:T(8,128)(2,1)}), bf16[128,2048]{1,0:T(8,128)(2,1)}) %reduce-scatter.10.cloned.1.call-update) | async-done | bytes 524304
  517.3 2.0 copy.17
  (14 shorter events, 0.1 us)
Async XLA Ops:
  7.2 45.8 %all-gather.5.cloned.1.call-start = ((), (), s32[]{:S(2)}) async-start(), calls=%async_computation.3 | async-start | bytes 1179648 | tf_op jit(solution)/shard_map/all_gather | solution.py:40
  7.9 142.2 %all-reduce.6.cloned.1.call-start = ((), (), s32[]{:S(2)}) async-start(), calls=%async_computation.11 | async-start | bytes 7340032 | tf_op jit(solution)/shard_map/psum | solution.py:48
  53.0 10.8 %copy-start = (bf16[256,2048]{1,0:T(8,128)(2,1)S(1)}, bf16[256,2048]{1,0:T(8,128)(2,1)}, u32[]{:S(2)}) copy-start(bf16[256,2048]{1,0:T(8,128)(2,1)} %all-gather.5.cloned.1.call-done) | copy-start | bytes 3145732
  74.1 151.5 %reduce-scatter.6.cloned.1.call-start = ((), (), s32[]{:S(2)}) async-start(), calls=%async_computation.4 | async-start | bytes 1179648 | tf_op jit(solution)/shard_map/reduce_scatter | solution.py:56
  150.1 75.4 %copy-start.3 = (bf16[32,2048]{1,0:T(8,128)(2,1)S(1)}, bf16[32,2048]{1,0:T(8,128)(2,1)}, u32[]{:S(2)}) copy-start(bf16[32,2048]{1,0:T(8,128)(2,1)} %param.6) | copy-start | bytes 393220
  161.7 130.6 %copy-start.4 = (s32[256]{0:T(256)S(1)}, s32[256]{0:T(256)}, u32[]{:S(2)}) copy-start(s32[256]{0:T(256)} %param.11) | copy-start | bytes 3076
  161.8 98.6 %all-reduce.4.cloned.1.call-start = ((), (), s32[]{:S(2)}) async-start(), calls=%async_computation.5 | async-start | bytes 131072 | tf_op jit(solution)/shard_map/psum | solution.py:63
  226.5 154.8 %copy-start.2 = (bf16[32,2048]{1,0:T(8,128)(2,1)}, bf16[32,2048]{1,0:T(8,128)(2,1)S(1)}, u32[]{:S(2)}) copy-start(bf16[32,2048]{1,0:T(8,128)(2,1)S(1)} %add_convert_fusion) | copy-start | bytes 393220
  230.2 107.9 %all-gather.7.cloned.1.call-start = ((), (), s32[]{:S(2)}) async-start(), calls=%async_computation.6 | async-start | bytes 1179648 | tf_op jit(solution)/shard_map/all_gather | solution.py:82
  297.8 79.7 %reduce-scatter.8.cloned.1.call-start = ((), (), s32[]{:S(2)}) async-start(), calls=%async_computation.7 | async-start | bytes 2293760 | tf_op jit(solution)/shard_map/reduce_scatter | solution.py:85
  348.8 4.0 copy-start.1
  348.8 54.7 %all-gather.9.cloned.1.call-start = ((), (), s32[]{:S(2)}) async-start(), calls=%async_computation.8 | async-start | bytes 2293760 | tf_op jit(solution)/shard_map/all_gather | solution.py:94
  380.4 50.7 %all-gather.11.cloned.1.call-start = ((), (), s32[]{:S(2)}) async-start(), calls=%async_computation.9 | async-start | bytes 2293760 | tf_op jit(solution)/shard_map/all_gather | solution.py:95
  381.2 136.1 %reduce-scatter.10.cloned.1.call-start = ((), (), s32[]{:S(2)}) async-start(), calls=%async_computation.10 | async-start | bytes 4718592
Sparse Core Ops, SparseCore 0:
  10.1 42.8 all-gather.4
  74.2 75.9 all-reduce.5
  161.9 63.6 reduce-scatter.5
  230.3 30.0 all-reduce.3
  297.9 40.0 all-gather.6
  348.9 28.5 reduce-scatter.7
  380.6 21.1 all-gather.8
  403.9 21.1 all-gather.10
  429.2 88.0 reduce-scatter.9
where the time goes:
time: 528 us; the launch traced here: 527 us
  waiting for transfers between devices  337 us (64%)
  matrix products  84.9 us (16%)
  local copies, waits for them, and re-layouts  46 us (9%)
  blocking collectives  31.6 us (6%)
  between operations  15.7 us (3%)
  other arithmetic  10.8 us (2%)
    psum x1, waiting for transfers between devices, per_device(): lax.psum(jnp.dot(rows_all, w_up, preferred_element_type=jnp.float32).asty...  76 us
    reduce_scatter x1, waiting for transfers between devices, per_device(): lax.psum_scatter(jnp.dot(picked, w_down, preferred_element_type=jnp.float...  63.7 us
    unnamed x10, waiting for transfers between devices  60 us
    unnamed x14, local copies, waits for them, and re-layouts  46 us
    all_gather x1, waiting for transfers between devices, per_device(): rows_all = lax.all_gather(tokens, 'gy', axis=0, tiled=True)  45.1 us
    all_gather x1, waiting for transfers between devices, per_device(): block_grads = lax.all_gather(grad_block, 'gy', axis=0, tiled=True)  40 us
    dot_general x5, matrix products, contract_lead(): lax.dot_general(left_mat, right_mat, (((0,), (0,)), ((), ())), preferred_...  33.1 us
    all_gather x1, blocking collectives, per_device(): proj_all = lax.all_gather(projected, 'gy', axis=0, tiled=True)  31.6 us
  transfers between devices with their start and end apart: 9, of which 7 were waited for; matrix products, arithmetic and copies ran while one was open for 16% of the time, Pallas kernels for 0%

commit v1 on v0

--- a/solution.py
+++ b/solution.py
@@ -79,7 +79,13 @@
         scatter_dimension=1,
         tiled=True,
     )
-    block_grads = lax.all_gather(grad_block, "gy", axis=0, tiled=True)
+    size = lax.axis_size("gy")
+    held, shards = (grad_block, [grad_block])
+    for _ in range(size - 1):
+        held = lax.ppermute(held, "gy", [(i, (i + 1) % size) for i in range(size)])
+        shards.insert(0, held)
+    row_of_blocks = jnp.concatenate(shards, axis=0)
+    block_grads = jnp.roll(row_of_blocks, (lax.axis_index("gy") + 1) * grad_block.shape[0], axis=0)
     grad_down = contract_lead(hidden_all, block_grads).astype(jnp.bfloat16)
     picked = block_grads
     grad_hidden = lax.psum_scatter(

time: 528 us -> 551 us (1.044)
  waiting for transfers between devices: 337 us -> 348 us
  local copies, waits for them, and re-layouts: 46 us -> 56.6 us
    ppermute x0 -> x7, waiting for transfers between devices: none -> 53.2 us  [per_device(): held = lax.ppermute(held, 'gy', [(i, (i + 1) % size) for i in range(size)])]
    all_gather x1 -> x0, waiting for transfers between devices: 40 us -> none  [per_device(): block_grads = lax.all_gather(grad_block, 'gy', axis=0, tiled=True)]
    unnamed x14 -> x29, local copies, waits for them, and re-layouts: 46 us -> 56 us
    unnamed x10 -> x9, waiting for transfers between devices: 60 us -> 59.8 us
  transfers between devices with their start and end apart: 9 -> 15, of which waited for: 7 -> 13; matrix products, arithmetic and copies ran while one was open for 16% -> 15% of each run, Pallas kernels for 0% -> 0%
where the time goes in v1:
time: 551 us; the launch traced here: 549 us
  waiting for transfers between devices  348 us (63%)
  matrix products  84.3 us (15%)
  local copies, waits for them, and re-layouts  56.6 us (10%)
  blocking collectives  31.6 us (6%)
  between operations  16 us (3%)
  other arithmetic  10.8 us (2%)
    psum x1, waiting for transfers between devices, per_device(): lax.psum(jnp.dot(rows_all, w_up, preferred_element_type=jnp.float32).asty...  76 us
    reduce_scatter x1, waiting for transfers between devices, per_device(): lax.psum_scatter(jnp.dot(picked, w_down, preferred_element_type=jnp.float...  63.7 us
    unnamed x9, waiting for transfers between devices  59.8 us
    unnamed x29, local copies, waits for them, and re-layouts  56 us
    ppermute x7, waiting for transfers between devices, per_device(): held = lax.ppermute(held, 'gy', [(i, (i + 1) % size) for i in range(size)])  53.2 us
    all_gather x1, waiting for transfers between devices, per_device(): rows_all = lax.all_gather(tokens, 'gy', axis=0, tiled=True)  45.1 us
    dot_general x5, matrix products, contract_lead(): lax.dot_general(left_mat, right_mat, (((0,), (0,)), ((), ())), preferred_...  33.1 us
    all_gather x1, blocking collectives, per_device(): proj_all = lax.all_gather(projected, 'gy', axis=0, tiled=True)  31.6 us
  transfers between devices with their start and end apart: 15, of which 13 were waited for; matrix products, arithmetic and copies ran while one was open for 15% of the time, Pallas kernels for 0%

profile of v1, /device:TPU:0, one launch (start us, length us, event | category | flops | bytes accessed | tf_op | source)
XLA Modules:
  0.0 549.2 jit_solution(2777856035686114903)
XLA Ops:
  7.2 0.7 all-gather.4.cloned.1.call-update
  7.9 45.1 %all-gather.4.cloned.1.call-done = bf16[256,2048]{1,0:T(8,128)(2,1)} async-done(((bf16[32,2048]{1,0:T(8,128)(2,1)}), bf16[256,2048]{1,0:T(8,128)(2,1)}) %all-gather.4.cloned.1.call-update) | async-done | bytes 1048592 | tf_op jit(solution)/shard_map/all_gather | solution.py:40
  53.0 10.8 %convolution_convert_fusion.4 = bf16[256,3584]{1,0:T(8,128)(2,1)} fusion(bf16[256,2048]{1,0:T(8,128)(2,1)} %all-gather.4.cloned.1.call-done, bf16[2048,3584]{1,0:T(8,128)(2,1)} %param.8), kind=kOutput, calls=%fused_computation.6 | convolution fusion | flops 3759013888 | bytes 17563648 | tf_op jit(solution)/shard_map/dot_general | solution.py:49
  63.8 10.3 %convolution_convert_fusion.5 = bf16[256,3584]{1,0:T(8,128)(2,1)} fusion(bf16[256,2048]{1,0:T(8,128)(2,1)S(1)} %copy-done, bf16[2048,3584]{1,0:T(8,128)(2,1)} %param.7), kind=kOutput, calls=%fused_computation.7 | convolution fusion | flops 3759013888 | bytes 17563648 | tf_op jit(solution)/shard_map/dot_general | solution.py:46
  74.1 76.0 %all-reduce.6.cloned.1.call-done = (bf16[256,3584]{1,0:T(8,128)(2,1)}, bf16[256,3584]{1,0:T(8,128)(2,1)}) async-done(((bf16[256,3584]{1,0:T(8,128)(2,1)}, bf16[256,3584]{1,0:T(8,128)(2,1)}), (bf16[256,3584]{1,0:T(8,128)(2,1)}, bf16[256,3584]{1,0:T(8,128)(2,1)})) %all-reduce.6.cloned.1.call-update) | async-done | bytes 3670032 | tf_op jit(solution)/shard_map/psum | solution.py:48
  150.1 11.6 %convolution_convert_fusion.7 = bf16[256,2048]{1,0:T(8,128)(2,1)} fusion(bf16[3584,2048]{1,0:T(8,128)(2,1)} %param.9, bf16[256,3584]{1,0:T(8,128)(2,1)} %get-tuple-element.20, bf16[256,3584]{1,0:T(8,128)(2,1)} %get-tuple-element.21), kind=kOutput, calls=%fused_computation.10 | convolution fusion | flops 3765960704 | bytes 19398656 | tf_op jit(solution)/shard_map/dot_general | solution.py:57
  161.8 63.7 %reduce-scatter.6.cloned.1.call-done = bf16[32,2048]{1,0:T(8,128)(2,1)} async-done(((bf16[256,2048]{1,0:T(8,128)(2,1)}), bf16[32,2048]{1,0:T(8,128)(2,1)}) %reduce-scatter.6.cloned.1.call-update) | async-done | bytes 131088 | tf_op jit(solution)/shard_map/reduce_scatter | solution.py:56
  225.5 0.9 add_convert_fusion
  226.5 3.7 convolution_convert_fusion.9
  230.3 30.2 %all-reduce.4.cloned.1.call-done = bf16[32,1024]{1,0:T(8,128)(2,1)} async-done(((bf16[32,1024]{1,0:T(8,128)(2,1)}), bf16[32,1024]{1,0:T(8,128)(2,1)}) %all-reduce.4.cloned.1.call-update) | async-done | bytes 65552 | tf_op jit(solution)/shard_map/psum | solution.py:63
  260.4 31.6 %all_gather.13 = bf16[256,1024]{1,0:T(8,128)(2,1)S(1)} all-gather(bf16[32,1024]{1,0:T(8,128)(2,1)} %all-reduce.4.cloned.1.call-done), channel_id=1, replica_groups=mesh['gx'=4,'gy'=8] {'gy'}, dimensions={0}, use_global_device_ids=true | all-gather | bytes 589824 | tf_op jit(solution)/shard_map/all_gather | solution.py:66
  293.6 3.5 convolution_convert_fusion.8
  297.2 1.5 collective-permute-start
  298.6 6.2 %collective-permute-done = bf16[32,2048]{1,0:T(8,128)(2,1)S(1)} collective-permute-done((bf16[32,2048]{1,0:T(8,128)(2,1)S(1)}, bf16[32,2048]{1,0:T(8,128)(2,1)S(1)}, u32[]{:S(2)}, u32[]{:S(2)}) %collective-permute-start) | collective-permute-done | bytes 131104 | tf_op jit(solution)/shard_map/ppermute | solution.py:85
  304.8 7.7 %collective-permute-done.1 = bf16[32,2048]{1,0:T(8,128)(2,1)S(1)} collective-permute-done((bf16[32,2048]{1,0:T(8,128)(2,1)S(1)}, bf16[32,2048]{1,0:T(8,128)(2,1)S(1)}, u32[]{:S(2)}, u32[]{:S(2)}) %collective-permute-start.1) | collective-permute-done | bytes 131104 | tf_op jit(solution)/shard_map/ppermute | solution.py:85
  312.5 7.7 %collective-permute-done.2 = bf16[32,2048]{1,0:T(8,128)(2,1)S(1)} collective-permute-done((bf16[32,2048]{1,0:T(8,128)(2,1)S(1)}, bf16[32,2048]{1,0:T(8,128)(2,1)S(1)}, u32[]{:S(2)}, u32[]{:S(2)}) %collective-permute-start.2) | collective-permute-done | bytes 131104 | tf_op jit(solution)/shard_map/ppermute | solution.py:85
  320.2 7.7 %collective-permute-done.3 = bf16[32,2048]{1,0:T(8,128)(2,1)S(1)} collective-permute-done((bf16[32,2048]{1,0:T(8,128)(2,1)S(1)}, bf16[32,2048]{1,0:T(8,128)(2,1)S(1)}, u32[]{:S(2)}, u32[]{:S(2)}) %collective-permute-start.3) | collective-permute-done | bytes 131104 | tf_op jit(solution)/shard_map/ppermute | solution.py:85
  327.8 8.7 %collective-permute-done.4 = bf16[32,2048]{1,0:T(8,128)(2,1)S(1)} collective-permute-done((bf16[32,2048]{1,0:T(8,128)(2,1)S(1)}, bf16[32,2048]{1,0:T(8,128)(2,1)S(1)}, u32[]{:S(2)}, u32[]{:S(2)}) %collective-permute-start.4) | collective-permute-done | bytes 131104 | tf_op jit(solution)/shard_map/ppermute | solution.py:85
  336.6 7.7 %collective-permute-done.5 = bf16[32,2048]{1,0:T(8,128)(2,1)S(1)} collective-permute-done((bf16[32,2048]{1,0:T(8,128)(2,1)S(1)}, bf16[32,2048]{1,0:T(8,128)(2,1)S(1)}, u32[]{:S(2)}, u32[]{:S(2)}) %collective-permute-start.5) | collective-permute-done | bytes 131104 | tf_op jit(solution)/shard_map/ppermute | solution.py:85
  344.2 7.7 %collective-permute-done.6 = bf16[32,2048]{1,0:T(8,128)(2,1)S(1)} collective-permute-done((bf16[32,2048]{1,0:T(8,128)(2,1)S(1)}, bf16[32,2048]{1,0:T(8,128)(2,1)S(1)}, u32[]{:S(2)}, u32[]{:S(2)}) %collective-permute-start.6) | collective-permute-done | bytes 131104 | tf_op jit(solution)/shard_map/ppermute | solution.py:85
  351.9 0.7 constant_dynamic-update-slice_fusion.15
  352.6 0.7 constant_dynamic-update-slice_fusion.14
  353.2 0.7 constant_dynamic-update-slice_fusion.13
  353.9 0.7 constant_dynamic-update-slice_fusion.12
  354.6 0.7 constant_dynamic-update-slice_fusion.11
  355.2 0.7 constant_dynamic-update-slice_fusion.10
  355.9 0.7 constant_dynamic-update-slice_fusion.9
  356.6 0.7 constant_dynamic-update-slice_fusion.8
  357.2 0.7 constant_dynamic-update-slice_fusion.7
  357.9 0.7 constant_dynamic-update-slice_fusion.6
  358.6 0.7 constant_dynamic-update-slice_fusion.5
  359.2 0.7 constant_dynamic-update-slice_fusion.4
  359.9 0.7 constant_dynamic-update-slice_fusion.3
  362.5 10.7 %convolution_convert_fusion.3 = bf16[256,3584]{1,0:T(8,128)(2,1)} fusion(bf16[3584,2048]{1,0:T(8,128)(2,1)} %param.9, bf16[512,2048]{1,0:T(8,128)(2,1)} %constant_dynamic-update-slice_fusion, s32[]{:T(128)S(6)} %select_n.33), kind=kOutput, calls=%fused_computation.5 | convolution fusion | flops 3759013888 | bytes 17563652 | tf_op jit(solution)/shard_map/dot_general | solution.py:15
  373.4 3.9 convert_element_type.74
  377.3 2.3 convert_element_type.76
  379.6 20.0 %reduce-scatter.8.cloned.1.call-done = bf16[64,3584]{1,0:T(8,128)(2,1)} async-done(((bf16[256,3584]{1,0:T(8,128)(2,1)}), bf16[64,3584]{1,0:T(8,128)(2,1)}) %reduce-scatter.8.cloned.1.call-update) | async-done | bytes 458768 | tf_op jit(solution)/shard_map/reduce_scatter | solution.py:91
  399.5 2.9 fusion.11
  402.6 0.7 all-gather.8.cloned.1.call-update
  403.3 3.3 convolution_convert_fusion.6
  406.6 6.5 %copy.16 = bf16[2048,1024]{0,1:T(8,128)(2,1)} copy(bf16[2048,1024]{1,0:T(8,128)(2,1)} %convolution_convert_fusion.6) | data formatting | bytes 8388608
  413.8 11.7 %convolution_convert_fusion = bf16[3584,2048]{1,0:T(8,128)(2,1)} fusion(bf16[512,2048]{1,0:T(8,128)(2,1)} %constant_dynamic-update-slice_fusion, s32[]{:T(128)S(6)} %select_n.33, bf16[256,3584]{1,0:T(8,128)(2,1)S(1)} %copy-done.1, bf16[256,3584]{1,0:T(8,128)(2,1)} %get-tuple-element.21), kind=kOutput, calls=%fused_computation | convolution fusion | flops 3772776448 | bytes 19398660 | tf_op jit(solution)/shard_map/dot_general | solution.py:9
  425.5 9.1 %fusion = bf16[2048,3584]{0,1:T(8,128)(2,1)} fusion(bf16[256,3584]{1,0:T(8,128)(2,1)} %all-gather.6.cloned.1.call-done, bf16[256,2048]{1,0:T(8,128)(2,1)S(1)} %copy-done), kind=kOutput, calls=%fused_computation.3 | convolution fusion | flops 3765436416 | bytes 17563648 | tf_op jit(solution)/shard_map/dot_general | solution.py:9
  434.6 18.7 %copy.14 = bf16[2048,3584]{1,0:T(8,128)(2,1)} copy(bf16[2048,3584]{0,1:T(8,128)(2,1)} %fusion) | data formatting | bytes 29360128
  453.3 8.8 %fusion.1 = bf16[2048,3584]{0,1:T(8,128)(2,1)} fusion(bf16[256,3584]{1,0:T(8,128)(2,1)} %all-gather.8.cloned.1.call-done, bf16[256,2048]{1,0:T(8,128)(2,1)S(1)} %copy-done), kind=kOutput, calls=%fused_computation.4 | convolution fusion | flops 3765436416 | bytes 17563648 | tf_op jit(solution)/shard_map/dot_general | solution.py:9
  462.0 18.8 %copy.15 = bf16[2048,3584]{1,0:T(8,128)(2,1)} copy(bf16[2048,3584]{0,1:T(8,128)(2,1)} %fusion.1) | data formatting | bytes 29360128
  480.8 58.4 %reduce-scatter.10.cloned.1.call-done = bf16[128,2048]{1,0:T(8,128)(2,1)} async-done(((bf16[1024,2048]{1,0:T(8,128)(2,1)}), bf16[128,2048]{1,0:T(8,128)(2,1)}) %reduce-scatter.10.cloned.1.call-update) | async-done | bytes 524304
  539.2 2.0 copy.17
  (41 shorter events, 4.1 us)
Async XLA Ops:
  7.2 45.8 %all-gather.4.cloned.1.call-start = ((), (), s32[]{:S(2)}) async-start(), calls=%async_computation.3 | async-start | bytes 1179648 | tf_op jit(solution)/shard_map/all_gather | solution.py:40
  7.9 142.2 %all-reduce.6.cloned.1.call-start = ((), (), s32[]{:S(2)}) async-start(), calls=%async_computation.10 | async-start | bytes 7340032 | tf_op jit(solution)/shard_map/psum | solution.py:48
  53.0 10.8 %copy-start = (bf16[256,2048]{1,0:T(8,128)(2,1)S(1)}, bf16[256,2048]{1,0:T(8,128)(2,1)}, u32[]{:S(2)}) copy-start(bf16[256,2048]{1,0:T(8,128)(2,1)} %all-gather.4.cloned.1.call-done) | copy-start | bytes 3145732
  74.1 151.5 %reduce-scatter.6.cloned.1.call-start = ((), (), s32[]{:S(2)}) async-start(), calls=%async_computation.4 | async-start | bytes 1179648 | tf_op jit(solution)/shard_map/reduce_scatter | solution.py:56
  150.1 75.4 %copy-start.3 = (bf16[32,2048]{1,0:T(8,128)(2,1)S(1)}, bf16[32,2048]{1,0:T(8,128)(2,1)}, u32[]{:S(2)}) copy-start(bf16[32,2048]{1,0:T(8,128)(2,1)} %param.6) | copy-start | bytes 393220
  161.7 98.7 %all-reduce.4.cloned.1.call-start = ((), (), s32[]{:S(2)}) async-start(), calls=%async_computation.5 | async-start | bytes 131072 | tf_op jit(solution)/shard_map/psum | solution.py:63
  226.5 176.9 %copy-start.2 = (bf16[32,2048]{1,0:T(8,128)(2,1)}, bf16[32,2048]{1,0:T(8,128)(2,1)S(1)}, u32[]{:S(2)}) copy-start(bf16[32,2048]{1,0:T(8,128)(2,1)S(1)} %add_convert_fusion) | copy-start | bytes 393220
  226.5 65.9 %copy-start.4 = (s32[256]{0:T(256)S(1)}, s32[256]{0:T(256)}, u32[]{:S(2)}) copy-start(s32[256]{0:T(256)} %param.11) | copy-start | bytes 3076
  230.2 169.3 %reduce-scatter.8.cloned.1.call-start = ((), (), s32[]{:S(2)}) async-start(), calls=%async_computation.6 | async-start | bytes 2293760 | tf_op jit(solution)/shard_map/reduce_scatter | solution.py:91
  297.2 7.7 %collective-permute-start = (bf16[32,2048]{1,0:T(8,128)(2,1)S(1)}, bf16[32,2048]{1,0:T(8,128)(2,1)S(1)}, u32[]{:S(2)}, u32[]{:S(2)}) collective-permute-start(bf16[32,2048]{1,0:T(8,128)(2,1)S(1)} %convolution_convert_fusion.8), channel_id=1, source_target_pairs={{0,1},{1,2},{2,3},{3,4},{4,5},{5,6},{6,7},{7,0},{8,9},{9,10},{10,1... | collective-permute-start | bytes 393224 | tf_op jit(solution)/shard_map/ppermute | solution.py:85
  304.8 7.7 %collective-permute-start.1 = (bf16[32,2048]{1,0:T(8,128)(2,1)S(1)}, bf16[32,2048]{1,0:T(8,128)(2,1)S(1)}, u32[]{:S(2)}, u32[]{:S(2)}) collective-permute-start(bf16[32,2048]{1,0:T(8,128)(2,1)S(1)} %collective-permute-done), channel_id=1, source_target_pairs={{0,1},{1,2},{2,3},{3,4},{4,5},{5,6},{6,7},{7,0},{8,9},{9,10},{10,1... | collective-permute-start | bytes 393224 | tf_op jit(solution)/shard_map/ppermute | solution.py:85
  312.5 7.7 %collective-permute-start.2 = (bf16[32,2048]{1,0:T(8,128)(2,1)S(1)}, bf16[32,2048]{1,0:T(8,128)(2,1)S(1)}, u32[]{:S(2)}, u32[]{:S(2)}) collective-permute-start(bf16[32,2048]{1,0:T(8,128)(2,1)S(1)} %collective-permute-done.1), channel_id=1, source_target_pairs={{0,1},{1,2},{2,3},{3,4},{4,5},{5,6},{6,7},{7,0},{8,9},{9,10},{10,1... | collective-permute-start | bytes 393224 | tf_op jit(solution)/shard_map/ppermute | solution.py:85
  320.2 7.7 %collective-permute-start.3 = (bf16[32,2048]{1,0:T(8,128)(2,1)S(1)}, bf16[32,2048]{1,0:T(8,128)(2,1)S(1)}, u32[]{:S(2)}, u32[]{:S(2)}) collective-permute-start(bf16[32,2048]{1,0:T(8,128)(2,1)S(1)} %collective-permute-done.2), channel_id=1, source_target_pairs={{0,1},{1,2},{2,3},{3,4},{4,5},{5,6},{6,7},{7,0},{8,9},{9,10},{10,1... | collective-permute-start | bytes 393224 | tf_op jit(solution)/shard_map/ppermute | solution.py:85
  327.8 8.7 %collective-permute-start.4 = (bf16[32,2048]{1,0:T(8,128)(2,1)S(1)}, bf16[32,2048]{1,0:T(8,128)(2,1)S(1)}, u32[]{:S(2)}, u32[]{:S(2)}) collective-permute-start(bf16[32,2048]{1,0:T(8,128)(2,1)S(1)} %collective-permute-done.3), channel_id=1, source_target_pairs={{0,1},{1,2},{2,3},{3,4},{4,5},{5,6},{6,7},{7,0},{8,9},{9,10},{10,1... | collective-permute-start | bytes 393224 | tf_op jit(solution)/shard_map/ppermute | solution.py:85
  336.6 7.7 %collective-permute-start.5 = (bf16[32,2048]{1,0:T(8,128)(2,1)S(1)}, bf16[32,2048]{1,0:T(8,128)(2,1)S(1)}, u32[]{:S(2)}, u32[]{:S(2)}) collective-permute-start(bf16[32,2048]{1,0:T(8,128)(2,1)S(1)} %collective-permute-done.4), channel_id=1, source_target_pairs={{0,1},{1,2},{2,3},{3,4},{4,5},{5,6},{6,7},{7,0},{8,9},{9,10},{10,1... | collective-permute-start | bytes 393224 | tf_op jit(solution)/shard_map/ppermute | solution.py:85
  344.2 7.7 %collective-permute-start.6 = (bf16[32,2048]{1,0:T(8,128)(2,1)S(1)}, bf16[32,2048]{1,0:T(8,128)(2,1)S(1)}, u32[]{:S(2)}, u32[]{:S(2)}) collective-permute-start(bf16[32,2048]{1,0:T(8,128)(2,1)S(1)} %collective-permute-done.5), channel_id=1, source_target_pairs={{0,1},{1,2},{2,3},{3,4},{4,5},{5,6},{6,7},{7,0},{8,9},{9,10},{10,1... | collective-permute-start | bytes 393224 | tf_op jit(solution)/shard_map/ppermute | solution.py:85
  373.3 52.2 %all-gather.6.cloned.1.call-start = ((), (), s32[]{:S(2)}) async-start(), calls=%async_computation.7 | async-start | bytes 2293760 | tf_op jit(solution)/shard_map/all_gather | solution.py:100
  373.4 3.9 copy-start.1
  402.5 50.8 %all-gather.8.cloned.1.call-start = ((), (), s32[]{:S(2)}) async-start(), calls=%async_computation.8 | async-start | bytes 2293760 | tf_op jit(solution)/shard_map/all_gather | solution.py:101
  403.3 135.9 %reduce-scatter.10.cloned.1.call-start = ((), (), s32[]{:S(2)}) async-start(), calls=%async_computation.9 | async-start | bytes 4718592
Sparse Core Ops, SparseCore 0:
  10.1 42.8 all-gather.3
  74.2 75.9 all-reduce.5
  161.9 63.6 reduce-scatter.5
  230.3 30.0 all-reduce.3
  373.4 26.0 reduce-scatter.7
  402.6 21.1 all-gather.5
  426.0 21.1 all-gather.7
  451.2 87.9 reduce-scatter.9
